TPU v7x, 512 devices: a whole 4x8x8 slice. The times are simulated.
512 devices in a mesh: dp: 16 (over y, core), lat: 32 (over z, x).
Axes of the slice: x: 4, y: 8, z: 8, core: 2. Of those that a mesh axis runs over, the one named last changes fastest.
Arguments:
- fields: bfloat16 [16, 96, 180, 768], P('dp', 'lat'), may hold values from -6 to 6
- cotangent: bfloat16 [16, 96, 180, 768], P('dp', 'lat'), may hold values from -6 to 6
- w_first: bfloat16 [2, 8, 96, 96], replicated, may hold values from -0.4375 to 0.4375
- b_first: float32 [2, 768], replicated, may hold values from -3 to 3
- w_second: bfloat16 [2, 8, 96, 96], replicated, may hold values from -0.4375 to 0.4375
- b_second: float32 [2, 768], replicated, may hold values from -3 to 3
Outputs:
- output: bfloat16 [16, 96, 180, 768], P('dp', 'lat')
- grad_fields: bfloat16 [16, 96, 180, 768], P('dp', 'lat')
- grad_w_first: float32 [2, 8, 96, 96], replicated
- grad_b_first: float32 [2, 768], replicated
- grad_w_second: float32 [2, 8, 96, 96], replicated
- grad_b_second: float32 [2, 768], replicated
All inputs are finite; a program needn't handle non-finite values.
Results may differ from a plain program's by a relative error of at most 0.015.
Values may be sent and summed in bfloat16 or wider, within the bound.
No kernel may reach another device: no remote copies, remote signals or barrier semaphores. Data moves between devices by JAX's collectives and lax.ppermute only.
A program may use at most 64 MiB of HBM per device.

v0:
```python
from functools import partial
import math
import jax
import jax.numpy as jnp
from jax import lax
from jax.sharding import PartitionSpec as P

C = 768
NB = 8
BS = 96
H = 96
W = 180
KX = 64
EPSILON = 1e-06


def layer_norm(values):
    centered = values - jnp.mean(values, axis=-1, keepdims=True)
    spread = jnp.mean(centered * centered, axis=-1, keepdims=True)
    return centered / jnp.sqrt(spread + EPSILON)


def angles(count_left, count_right, period):
    left_index = jnp.arange(count_left, dtype=jnp.int32)[:, None]
    right_index = jnp.arange(count_right, dtype=jnp.int32)[None, :]
    return 2.0 * math.pi / period * (left_index * right_index % period).astype(jnp.float32)


def longitude_tables(mode_count):
    angle_grid = angles(W, mode_count, W)
    mode_index = jnp.arange(mode_count, dtype=jnp.int32)[None, :]
    live_modes = jnp.where(mode_index <= W // 2, 1.0, 0.0).astype(jnp.float32) / math.sqrt(W)
    weight = jnp.where(mode_index == 0, 1.0, 2.0).astype(jnp.float32) * live_modes
    forward = jnp.stack(
        [jnp.cos(angle_grid) * live_modes, -jnp.sin(angle_grid) * live_modes], axis=2
    )
    inverse = jnp.stack([jnp.cos(angle_grid) * weight, -jnp.sin(angle_grid) * weight], axis=2)
    return (forward.astype(jnp.bfloat16), inverse.astype(jnp.bfloat16))


def latitude_table():
    angle_grid = angles(H, H, H)
    cosine = jnp.cos(angle_grid) / math.sqrt(H)
    sine_part = jnp.sin(angle_grid) / math.sqrt(H)
    real_row = jnp.stack([cosine, sine_part], axis=2)
    imag_row = jnp.stack([-sine_part, cosine], axis=2)
    return jnp.stack([real_row, imag_row], axis=1).astype(jnp.bfloat16)


def real_form(weight):
    real_part = weight[0]
    imag_part = weight[1]
    upper_rows = jnp.stack([real_part, imag_part], axis=2)
    lower_rows = jnp.stack([-imag_part, real_part], axis=2)
    return jnp.stack([upper_rows, lower_rows], axis=1)


def fold_grads(gathered):
    real_grad = gathered[:, 0, :, 0, :] + gathered[:, 1, :, 1, :]
    imag_grad = gathered[:, 0, :, 1, :] - gathered[:, 1, :, 0, :]
    return jnp.stack([real_grad, imag_grad], axis=0)


def product(pattern, left_side, right_side):
    return jnp.einsum(pattern, left_side, right_side, preferred_element_type=jnp.float32)


def spectral_forward(spectra_modes, first_form, bias_one, second_form, bias_two):
    leading = spectra_modes.shape[:3]
    blocked = spectra_modes.reshape(leading + (2, NB, BS))
    pre_one = (
        product("bmkqni,nqipo->bmkpno", blocked, first_form).reshape(leading + (2, C)) + bias_one
    )
    hidden = jax.nn.gelu(pre_one, approximate=False).astype(jnp.bfloat16)
    pre_two = (
        product("bmkqni,nqipo->bmkpno", hidden.reshape(leading + (2, NB, BS)), second_form).reshape(
            leading + (2, C)
        )
        + bias_two
    )
    return (pre_one, hidden, pre_two)


def spectral_backward(spectra_modes, pre_one, hidden, first_form, second_form, back_filtered):
    leading = spectra_modes.shape[:3]
    back_blocked = back_filtered.reshape(leading + (2, NB, BS))
    grad_second = product(
        "bmkqni,bmkpno->nqipo", hidden.reshape(leading + (2, NB, BS)), back_blocked
    )
    bias_two_grad = jnp.sum(back_filtered.astype(jnp.float32), axis=(0, 1, 2))
    back_hidden = product("bmkpno,nqipo->bmkqni", back_blocked, second_form).reshape(
        leading + (2, C)
    )
    unused, gelu_back = jax.vjp(partial(jax.nn.gelu, approximate=False), pre_one)
    back_pre = gelu_back(back_hidden)[0].astype(jnp.bfloat16)
    pre_blocked = back_pre.reshape(leading + (2, NB, BS))
    grad_first = product(
        "bmkqni,bmkpno->nqipo", spectra_modes.reshape(leading + (2, NB, BS)), pre_blocked
    )
    bias_one_grad = jnp.sum(back_pre.astype(jnp.float32), axis=(0, 1, 2))
    back_modes = (
        product("bmkpno,nqipo->bmkqni", pre_blocked, first_form)
        .reshape(leading + (2, C))
        .astype(jnp.bfloat16)
    )
    return (
        fold_grads(grad_first),
        bias_one_grad,
        fold_grads(grad_second),
        bias_two_grad,
        back_modes,
    )


def on_device(fields, cotangent, w_first, b_first, w_second, b_second):
    band_count = lax.axis_size("lat")
    mode_count = (W // 2 + band_count) // band_count * band_count
    local_modes = mode_count // band_count
    mode_index = lax.axis_index("lat") * local_modes + jnp.arange(local_modes, dtype=jnp.int32)
    mode_mask = (
        jnp.where(mode_index < KX, 1.0, 0.0).astype(jnp.float32).reshape(1, 1, local_modes, 1, 1)
    )
    forward_lon, inverse_lon = longitude_tables(mode_count)
    latitude = latitude_table()
    first_form = real_form(w_first)
    second_form = real_form(w_second)
    values = fields.astype(jnp.float32)
    normed, norm_back = jax.vjp(layer_norm, values)
    spectra = product("bhwc,wkp->bhkpc", normed.astype(jnp.bfloat16), forward_lon).astype(
        jnp.bfloat16
    )
    column_spectra = lax.all_to_all(spectra, "lat", split_axis=2, concat_axis=1, tiled=True)
    spectra_modes = product("mqhp,bhkpc->bmkqc", latitude, column_spectra).astype(jnp.bfloat16)
    pre_one, hidden, pre_two = spectral_forward(
        spectra_modes, first_form, b_first, second_form, b_second
    )
    filtered = (pre_two * mode_mask).astype(jnp.bfloat16)
    column_rows = product("mphq,bmkpc->bhkqc", latitude, filtered).astype(jnp.bfloat16)
    row_spectra = lax.all_to_all(column_rows, "lat", split_axis=1, concat_axis=2, tiled=True)
    mixed = product("bhkpc,wkp->bhwc", row_spectra, inverse_lon)
    result = (values + normed + mixed).astype(jnp.bfloat16)
    upstream = cotangent.astype(jnp.float32)
    back_rows = product("bhwc,wkp->bhkpc", cotangent, inverse_lon).astype(jnp.bfloat16)
    back_columns = lax.all_to_all(back_rows, "lat", split_axis=2, concat_axis=1, tiled=True)
    back_filtered = (product("mphq,bhkqc->bmkpc", latitude, back_columns) * mode_mask).astype(
        jnp.bfloat16
    )
    grad_one, bias_one, grad_two, bias_two, back_modes = spectral_backward(
        spectra_modes, pre_one, hidden, first_form, second_form, back_filtered
    )
    back_column_rows = product("mqhp,bmkqc->bhkpc", latitude, back_modes).astype(jnp.bfloat16)
    back_spectra = lax.all_to_all(back_column_rows, "lat", split_axis=1, concat_axis=2, tiled=True)
    back_normed = upstream + product("bhkpc,wkp->bhwc", back_spectra, forward_lon)
    back_fields = (upstream + norm_back(back_normed)[0]).astype(jnp.bfloat16)
    grad_scale = 1.0 / (fields.shape[0] * lax.axis_size("dp") * H)
    members = (grad_one, bias_one, grad_two, bias_two)
    packed = jnp.concatenate([member.reshape(-1) for member in members]) * grad_scale
    all_grads = lax.psum(packed, ("dp", "lat"))
    results = []
    offset = 0
    for member in members:
        length = member.size
        results.append(all_grads[offset : offset + length].reshape(member.shape))
        offset = offset + length
    return (result, back_fields, results[0], results[1], results[2], results[3])


def solution(mesh):
    placed = (P("dp", "lat", None, None), P("dp", "lat", None, None), P(), P(), P(), P())
    return jax.shard_map(
        on_device,
        mesh=mesh,
        in_specs=placed,
        out_specs=(P("dp", "lat", None, None), P("dp", "lat", None, None), P(), P(), P(), P()),
        check_vma=False,
    )
```

profile of v0, /device:TPU:1, one launch (start us, length us, event | category | flops | bytes accessed | tf_op | source)
XLA Modules:
  0.0 435.8 jit_solution(13082725453070378187)
XLA Ops:
  8.5 1.6 fusion.34
  12.4 1.7 fusion.40
  14.1 1.8 copy.151
  16.0 13.7 %all-to-all-start = ((bf16[1,3,96,2,768]{4,3,1,0,2:T(2,128)(2,1)}), bf16[1,3,96,2,768]{4,3,1,0,2:T(2,128)(2,1)S(1)}, u32[]{:S(2)}, u32[]{:S(2)}) async-start(bf16[1,3,96,2,768]{4,3,1,0,2:T(2,128)(2,1)} %copy.151), calls=%async_computation | async-start | bytes 1769472 | tf_op jit(solution)/shard_map/all_to_all | solution.py:132
  31.2 1.8 copy.163
  33.1 19.5 %all-to-all-done = bf16[1,3,96,2,768]{4,3,1,0,2:T(2,128)(2,1)S(1)} async-done(((bf16[1,3,96,2,768]{4,3,1,0,2:T(2,128)(2,1)}), bf16[1,3,96,2,768]{4,3,1,0,2:T(2,128)(2,1)S(1)}, u32[]{:S(2)}, u32[]{:S(2)}) %all-to-all-start) | async-done | bytes 884768 | tf_op jit(solution)/shard_map/all_to_all | solution.py:132
  52.6 6.1 %all-to-all-start.2 = ((bf16[1,3,96,2,768]{4,3,1,0,2:T(2,128)(2,1)}), bf16[1,3,96,2,768]{4,3,1,0,2:T(2,128)(2,1)S(1)}, u32[]{:S(2)}, u32[]{:S(2)}) async-start(bf16[1,3,96,2,768]{4,3,1,0,2:T(2,128)(2,1)} %copy.163), calls=%async_computation.2 | async-start | bytes 1769472 | tf_op jit(solution)/shard_map/all_to_all | solution.py:144
  67.7 2.2 reshape.652
  69.9 10.8 %all-to-all-done.2 = bf16[1,3,96,2,768]{4,3,1,0,2:T(2,128)(2,1)S(1)} async-done(((bf16[1,3,96,2,768]{4,3,1,0,2:T(2,128)(2,1)}), bf16[1,3,96,2,768]{4,3,1,0,2:T(2,128)(2,1)S(1)}, u32[]{:S(2)}, u32[]{:S(2)}) %all-to-all-start.2) | async-done | bytes 884768 | tf_op jit(solution)/shard_map/all_to_all | solution.py:144
  83.4 2.4 reshape.658
  85.8 6.8 %fusion.5 = (f32[96,3,2,8,96]{4,0,1,2,3:T(8,128)S(1)}, f32[8,2,96,96,3,1]{2,3,5,4,1,0:T(8,128)S(1)}) fusion(f32[2,8,96]{2,0,1:T(2,128)S(1)} %copy-done.23, bf16[96,3,2,8,96,1]{4,3,0,2,1,5:T(8,128)(2,1)} %bitcast.367, bf16[8,1,96,2,96]{4,2,1,3,0:T(8,128)(2,1)S(1)} %copy-done.13, bf16[8,1,96,2,96]{4,2,1,3,0:T(8,128)(2,1)S(1)} %copy-done.11), kind=kOutput, calls=%fused_computation.11 | convolution fusion | flops 198918144 | bytes 5019648 | tf_op jit(solution)/shard_map/bmkqni,nqipo->bmkpno/dot_general | solution.py:65
  94.4 8.0 %convert_reduce_fusion.1 = (f32[2,8,96]{2,0,1:T(2,128)}, bf16[1,96,3,2,8,96]{5,1,2,3,4,0:T(8,128)(2,1)}, f32[1,96,3,2,8,96]{5,1,2,3,4,0:T(8,128)}, f32[8,2,96,96,3,1]{2,3,5,4,1,0:T(8,128)S(1)}) fusion(f32[2,8,96]{2,0,1:T(2,128)S(1)} %copy-done.23, f32[8,2,96,96,3,1]{2,3,5,4,1,0:T(8,128)S(1)} %get-tuple-element.35, ...), kind=kOutput, calls=%fused_computation.34 | convolution fusion | flops 203340288 | bytes 7680000 | tf_op jit(solution)/shard_map/bmkpno,nqipo->bmkqni/dot_general | solution.py:65
  102.5 1.7 convolution_bitcast_fusion.2
  107.8 3.2 convolution_bitcast_fusion
  111.0 2.0 copy.158
  113.0 2.1 reshape.654
  115.6 1.8 copy.160
  118.1 6.6 %all-to-all-start.1 = ((bf16[1,96,3,2,768]{4,3,2,0,1:T(2,128)(2,1)}), bf16[1,96,3,2,768]{4,3,2,0,1:T(2,128)(2,1)S(1)}, u32[]{:S(2)}, u32[]{:S(2)}) async-start(bf16[1,96,3,2,768]{4,3,2,0,1:T(2,128)(2,1)} %copy.160), calls=%async_computation.1 | async-start | bytes 1769472 | tf_op jit(solution)/shard_map/all_to_all | solution.py:139
  127.2 2.3 maximum_multiply_fusion
  129.6 2.9 fusion.39
  132.5 1.8 copy.171
  134.3 1.9 reshape.694
  136.2 1.6 fusion.45
  137.8 1.8 copy.173
  139.7 6.8 %all-to-all-done.1 = bf16[1,96,3,2,768]{4,3,2,0,1:T(2,128)(2,1)S(1)} async-done(((bf16[1,96,3,2,768]{4,3,2,0,1:T(2,128)(2,1)}), bf16[1,96,3,2,768]{4,3,2,0,1:T(2,128)(2,1)S(1)}, u32[]{:S(2)}, u32[]{:S(2)}) %all-to-all-start.1) | async-done | bytes 884768 | tf_op jit(solution)/shard_map/all_to_all | solution.py:139
  146.5 6.9 %all-to-all-start.3 = ((bf16[1,96,3,2,768]{4,3,2,0,1:T(2,128)(2,1)}), bf16[1,96,3,2,768]{4,3,2,0,1:T(2,128)(2,1)}, u32[]{:S(2)}, u32[]{:S(2)}) async-start(bf16[1,96,3,2,768]{4,3,2,0,1:T(2,128)(2,1)} %copy.173), calls=%async_computation.3 | async-start | bytes 1769472 | tf_op jit(solution)/shard_map/all_to_all | solution.py:152
  153.4 261.3 %all-reduce.2.cloned.1.call-done = f32[297984]{0:T(1024)} async-done(((f32[297984]{0:T(1024)}), f32[297984]{0:T(1024)}) %all-reduce.2.cloned.1.call-update) | async-done | bytes 1191952 | tf_op jit(solution)/shard_map/psum | solution.py:158
  414.7 2.1 fusion.121
  418.8 2.2 reshape.668
  422.8 1.4 fusion.37
  424.2 1.8 copy.174
  427.4 1.6 fusion.33
  (119 shorter events, 30.7 us)
Async XLA Ops:
  14.1 16.7 %copy-start.2 = (bf16[1,3,180,768]{3,2,1,0:T(8,128)(2,1)S(1)}, bf16[1,3,180,768]{3,2,1,0:T(8,128)(2,1)}, u32[]{:S(2)}) copy-start(bf16[1,3,180,768]{3,2,1,0:T(8,128)(2,1)} %param.7) | copy-start | bytes 2488324
  16.0 36.7 %all-to-all-start = ((bf16[1,3,96,2,768]{4,3,1,0,2:T(2,128)(2,1)}), bf16[1,3,96,2,768]{4,3,1,0,2:T(2,128)(2,1)S(1)}, u32[]{:S(2)}, u32[]{:S(2)}) async-start(bf16[1,3,96,2,768]{4,3,1,0,2:T(2,128)(2,1)} %copy.151), calls=%async_computation | async-start | bytes 1769472 | tf_op jit(solution)/shard_map/all_to_all | solution.py:132
  31.2 28.6 %copy-start.30 = (f32[2,768]{1,0:T(2,128)S(1)}, f32[2,768]{1,0:T(2,128)}, u32[]{:S(2)}) copy-start(f32[2,768]{1,0:T(2,128)} %param.9) | copy-start | bytes 18436
  52.6 28.1 %all-to-all-start.2 = ((bf16[1,3,96,2,768]{4,3,1,0,2:T(2,128)(2,1)}), bf16[1,3,96,2,768]{4,3,1,0,2:T(2,128)(2,1)S(1)}, u32[]{:S(2)}, u32[]{:S(2)}) async-start(bf16[1,3,96,2,768]{4,3,1,0,2:T(2,128)(2,1)} %copy.163), calls=%async_computation.2 | async-start | bytes 1769472 | tf_op jit(solution)/shard_map/all_to_all | solution.py:144
  61.8 53.3 %copy-start.9 = (bf16[96,1,96,2]{2,0,3,1:T(8,128)(2,1)}, bf16[96,1,96,2]{2,0,3,1:T(8,128)(2,1)S(1)}, u32[]{:S(2)}) copy-start(bf16[96,1,96,2]{2,0,3,1:T(8,128)(2,1)S(1)} %get-tuple-element.22) | copy-start | bytes 110596
  62.8 31.5 %copy-start.4 = (bf16[8,1,96,2,96]{2,4,1,3,0:T(8,128)(2,1)}, bf16[8,1,96,2,96]{2,4,1,3,0:T(8,128)(2,1)S(1)}, u32[]{:S(2)}) copy-start(bf16[8,1,96,2,96]{2,4,1,3,0:T(8,128)(2,1)S(1)} %get-tuple-element.19) | copy-start | bytes 884740
  67.6 14.3 %copy-start.32 = (f32[3]{0:T(128)S(1)}, f32[3]{0:T(128)}, u32[]{:S(2)}) copy-start(f32[3]{0:T(128)} %compare_select_fusion) | copy-start | bytes 40
  82.0 3.8 copy-start.11
  82.0 3.8 copy-start.13
  82.0 3.8 copy-start.23
  92.6 9.9 %copy-start.1 = (f32[8,2,96,96,3,1]{2,3,5,4,1,0:T(8,128)}, f32[8,2,96,96,3,1]{2,3,5,4,1,0:T(8,128)S(1)}, u32[]{:S(2)}) copy-start(f32[8,2,96,96,3,1]{2,3,5,4,1,0:T(8,128)S(1)} %get-tuple-element.35) | copy-start | bytes 5308420
  93.4 1.0 copy-start.5
  94.4 8.0 %copy-start.8 = (bf16[96,3,2,8,96]{4,3,0,2,1:T(8,128)(2,1)S(1)}, bf16[96,3,2,8,96]{4,3,0,2,1:T(8,128)(2,1)}, u32[]{:S(2)}) copy-start(bf16[96,3,2,8,96]{4,3,0,2,1:T(8,128)(2,1)} %reshape.652) | copy-start | bytes 2654212
  104.2 2.2 copy-start.7
  113.0 2.1 copy-start.31
  115.1 2.3 copy-start.29
  115.6 9.2 %copy-start.6 = (f32[1,8,96,96]{3,2,1,0:T(8,128)S(1)}, f32[1,8,96,96]{3,2,1,0:T(8,128)}, u32[]{:S(2)}) copy-start(f32[1,8,96,96]{3,2,1,0:T(8,128)} %fusion.84) | copy-start | bytes 884740
  118.1 9.1 %copy-start.3 = (f32[147456]{0:T(1024)S(1)}, f32[147456]{0:T(1024)}, u32[]{:S(2)}) copy-start(f32[147456]{0:T(1024)} %reshape.665) | copy-start | bytes 1769476
  118.1 28.3 %all-to-all-start.1 = ((bf16[1,96,3,2,768]{4,3,2,0,1:T(2,128)(2,1)}), bf16[1,96,3,2,768]{4,3,2,0,1:T(2,128)(2,1)S(1)}, u32[]{:S(2)}, u32[]{:S(2)}) async-start(bf16[1,96,3,2,768]{4,3,2,0,1:T(2,128)(2,1)} %copy.160), calls=%async_computation.1 | async-start | bytes 1769472 | tf_op jit(solution)/shard_map/all_to_all | solution.py:139
  124.8 289.9 %all-reduce.2.cloned.1.call-start = ((), (), s32[]{:S(2)}) async-start(), calls=%async_computation.4 | async-start | bytes 2383872 | tf_op jit(solution)/shard_map/psum | solution.py:158
  125.9 3.6 copy-start.12
  127.2 2.4 copy-start.14
  132.5 3.7 copy-start.10
  146.5 277.8 %all-to-all-start.3 = ((bf16[1,96,3,2,768]{4,3,2,0,1:T(2,128)(2,1)}), bf16[1,96,3,2,768]{4,3,2,0,1:T(2,128)(2,1)}, u32[]{:S(2)}, u32[]{:S(2)}) async-start(bf16[1,96,3,2,768]{4,3,2,0,1:T(2,128)(2,1)} %copy.173), calls=%async_computation.3 | async-start | bytes 1769472 | tf_op jit(solution)/shard_map/all_to_all | solution.py:152
  416.8 5.9 %copy-start = (bf16[1,3,180,768]{3,2,1,0:T(8,128)(2,1)S(1)}, bf16[1,3,180,768]{3,2,1,0:T(8,128)(2,1)}, u32[]{:S(2)}) copy-start(bf16[1,3,180,768]{3,2,1,0:T(8,128)(2,1)} %param.6) | copy-start | bytes 2488324
  416.8 5.9 %copy-start.20 = (bf16[180,96,1]{1,0,2:T(8,128)(2,1)S(1)}, bf16[180,96,1]{1,0,2:T(8,128)(2,1)}, u32[]{:S(2)}) copy-start(bf16[180,96,1]{1,0,2:T(8,128)(2,1)} %copy-done.19) | copy-start | bytes 103684
  416.8 5.9 %copy-start.22 = (bf16[180,96,1]{1,0,2:T(8,128)(2,1)S(1)}, bf16[180,96,1]{1,0,2:T(8,128)(2,1)}, u32[]{:S(2)}) copy-start(bf16[180,96,1]{1,0,2:T(8,128)(2,1)} %copy-done.21) | copy-start | bytes 103684
  416.8 5.9 %copy-start.25 = (f32[3,180]{1,0:T(4,128)S(1)}, f32[3,180]{1,0:T(4,128)}, u32[]{:S(2)}) copy-start(f32[3,180]{1,0:T(4,128)} %copy-done.24) | copy-start | bytes 6484
  422.8 3.2 copy-start.16
  422.8 3.2 copy-start.18
  422.8 3.2 copy-start.28
  426.0 0.8 copy-start.27
  (6 other events, 3.7 us)
Sparse Core Ops, SparseCore 0:
  130.7 283.9 all-reduce.1
where the time goes:
time: 437 us; the launch traced here: 436 us
  waiting for transfers between devices  298 us (68%)
  local copies, waits for them, and re-layouts  41 us (9%)
  starting transfers between devices  33.5 us (8%)
  matrix products  31.7 us (7%)
  other arithmetic  16.5 us (4%)
  between operations  14.6 us (3%)
    psum x1, waiting for transfers between devices, on_device(): all_grads = lax.psum(packed, ('dp', 'lat'))  261 us
    dot_general x14, matrix products, product(): jnp.einsum(pattern, left_side, right_side, preferred_element_type=jnp.flo...  31.7 us
    all_to_all x1, waiting for transfers between devices, on_device(): lax.all_to_all(spectra, 'lat', split_axis=2, concat_axis=1, tiled=True)  19.5 us
    all_to_all x1, starting transfers between devices, on_device(): lax.all_to_all(spectra, 'lat', split_axis=2, concat_axis=1, tiled=True)  13.7 us
    all_to_all x1, waiting for transfers between devices, on_device(): lax.all_to_all(back_rows, 'lat', split_axis=2, concat_axis=1, tiled=True)  10.8 us
  transfers between devices with their start and end apart: 5, of which 4 were waited for; matrix products, arithmetic and copies ran while one was open for 9% of the time, Pallas kernels for 0%

commit v1 on v0

--- a/solution.py
+++ b/solution.py
@@ -129,7 +129,10 @@
     spectra = product("bhwc,wkp->bhkpc", normed.astype(jnp.bfloat16), forward_lon).astype(
         jnp.bfloat16
     )
-    column_spectra = lax.all_to_all(spectra, "lat", split_axis=2, concat_axis=1, tiled=True)
+    column_spectra = jnp.concatenate(
+        lax.all_to_all(jnp.stack(jnp.split(spectra, lax.axis_size("lat"), axis=2)), "lat", 0, 0),
+        axis=1,
+    )
     spectra_modes = product("mqhp,bhkpc->bmkqc", latitude, column_spectra).astype(jnp.bfloat16)
     pre_one, hidden, pre_two = spectral_forward(
         spectra_modes, first_form, b_first, second_form, b_second

time: 437 us -> 430 us (0.984)
    all_to_all x1, waiting for transfers between devices: 19.5 us -> 10.2 us  [on_device(): lax.all_to_all(jnp.stack(jnp.split(spectra, lax.axis_size('lat'), axis=2)...]
    all_to_all x1, starting transfers between devices: 13.7 us -> 6.14 us  [on_device(): lax.all_to_all(jnp.stack(jnp.split(spectra, lax.axis_size('lat'), axis=2)...]
    all_to_all x1, starting transfers between devices: 6.14 us -> 13.7 us  [on_device(): lax.all_to_all(back_rows, 'lat', split_axis=2, concat_axis=1, tiled=True)]
    all_to_all x1, waiting for transfers between devices: 10.8 us -> 17.7 us  [on_device(): lax.all_to_all(back_rows, 'lat', split_axis=2, concat_axis=1, tiled=True)]
where the time goes in v1:
time: 430 us; the launch traced here: 429 us
  waiting for transfers between devices  296 us (69%)
  local copies, waits for them, and re-layouts  38.4 us (9%)
  starting transfers between devices  33.5 us (8%)
  matrix products  33.2 us (8%)
  between operations  14.8 us (3%)
  other arithmetic  13.7 us (3%)
    psum x1, waiting for transfers between devices, on_device(): all_grads = lax.psum(packed, ('dp', 'lat'))  261 us
    dot_general x14, matrix products, product(): jnp.einsum(pattern, left_side, right_side, preferred_element_type=jnp.flo...  33.2 us
    all_to_all x1, waiting for transfers between devices, on_device(): lax.all_to_all(back_rows, 'lat', split_axis=2, concat_axis=1, tiled=True)  17.7 us
    all_to_all x1, starting transfers between devices, on_device(): lax.all_to_all(back_rows, 'lat', split_axis=2, concat_axis=1, tiled=True)  13.7 us
    all_to_all x1, waiting for transfers between devices, on_device(): lax.all_to_all(jnp.stack(jnp.split(spectra, lax.axis_size('lat'), axis=2)...  10.2 us
  transfers between devices with their start and end apart: 5, of which 4 were waited for; matrix products, arithmetic and copies ran while one was open for 9% of the time, Pallas kernels for 0%

profile of v1, /device:TPU:1, one launch (start us, length us, event | category | flops | bytes accessed | tf_op | source)
XLA Modules:
  0.0 429.1 jit_solution(5514507537022855947)
XLA Ops:
  8.2 1.7 fusion.41
  9.9 1.8 copy.155
  11.8 13.7 %all-to-all-start.2 = ((bf16[1,3,96,2,768]{4,3,1,0,2:T(2,128)(2,1)}), bf16[1,3,96,2,768]{4,3,1,0,2:T(2,128)(2,1)S(1)}, u32[]{:S(2)}, u32[]{:S(2)}) async-start(bf16[1,3,96,2,768]{4,3,1,0,2:T(2,128)(2,1)} %copy.155), calls=%async_computation.2 | async-start | bytes 1769472 | tf_op jit(solution)/shard_map/all_to_all | solution.py:147
  29.0 1.7 copy.145
  30.7 17.7 %all-to-all-done.2 = bf16[1,3,96,2,768]{4,3,1,0,2:T(2,128)(2,1)S(1)} async-done(((bf16[1,3,96,2,768]{4,3,1,0,2:T(2,128)(2,1)}), bf16[1,3,96,2,768]{4,3,1,0,2:T(2,128)(2,1)S(1)}, u32[]{:S(2)}, u32[]{:S(2)}) %all-to-all-start.2) | async-done | bytes 884768 | tf_op jit(solution)/shard_map/all_to_all | solution.py:147
  48.4 6.1 %all-to-all-start = ((bf16[32,1,3,3,2,768]{5,4,3,2,1,0:T(2,128)(2,1)}), bf16[32,1,3,3,2,768]{5,4,3,2,1,0:T(2,128)(2,1)S(1)}, u32[]{:S(2)}, u32[]{:S(2)}) async-start(bf16[32,1,3,3,2,768]{5,4,3,2,1,0:T(2,128)(2,1)} %copy.145), calls=%async_computation | async-start | bytes 1769472 | tf_op jit(solution)/shard_map/all_to_all | solution.py:133
  62.5 1.4 convert_reduce_fusion.2
  63.9 2.4 reshape.659
  66.3 10.2 %all-to-all-done = bf16[32,1,3,3,2,768]{5,4,3,2,1,0:T(2,128)(2,1)S(1)} async-done(((bf16[32,1,3,3,2,768]{5,4,3,2,1,0:T(2,128)(2,1)}), bf16[32,1,3,3,2,768]{5,4,3,2,1,0:T(2,128)(2,1)S(1)}, u32[]{:S(2)}, u32[]{:S(2)}) %all-to-all-start) | async-done | bytes 884768 | tf_op jit(solution)/shard_map/all_to_all | solution.py:133
  76.5 2.2 fusion.42
  78.7 3.2 reshape.653
  81.9 7.0 %fusion.5 = (f32[96,3,2,8,96]{4,0,1,2,3:T(8,128)S(1)}, f32[8,2,96,96,3,1]{2,3,5,4,1,0:T(8,128)S(1)}) fusion(f32[2,8,96]{2,0,1:T(2,128)S(1)} %copy-done.22, bf16[96,3,2,8,96,1]{4,3,0,2,1,5:T(8,128)(2,1)} %bitcast.491, bf16[8,1,96,2,96]{4,2,1,3,0:T(8,128)(2,1)} %get-tuple-element.18, bf16[8,1,96,2,96]{4,2,1,3,0:T(8,128)(2,1)} %get-tuple-element.17), kind=kOutput, calls=%fused_computation.11 | convolution fusion | flops 198918144 | bytes 5019648 | tf_op jit(solution)/shard_map/bmkqni,nqipo->bmkpno/dot_general | solution.py:65
  90.7 7.2 %convert_reduce_fusion.1 = (f32[2,8,96]{2,0,1:T(2,128)S(1)}, bf16[1,96,3,2,8,96]{5,1,2,3,4,0:T(8,128)(2,1)}, f32[1,96,3,2,8,96]{5,1,2,3,4,0:T(8,128)}, f32[8,2,96,96,3,1]{2,3,5,4,1,0:T(8,128)S(1)}) fusion(f32[2,8,96]{2,0,1:T(2,128)S(1)} %copy-done.22, f32[8,2,96,96,3,1]{2,3,5,4,1,0:T(8,128)S(1)} %get-tuple-element.35, ...), kind=kOutput, calls=%fused_computation.34 | convolution fusion | flops 203340288 | bytes 7680000 | tf_op jit(solution)/shard_map/bmkpno,nqipo->bmkqni/dot_general | solution.py:65
  97.9 1.9 convolution_bitcast_fusion.2
  103.5 3.2 convolution_bitcast_fusion
  106.7 2.0 copy.150
  108.7 2.1 reshape.655
  111.3 1.8 copy.152
  113.8 6.6 %all-to-all-start.1 = ((bf16[1,96,3,2,768]{4,3,2,0,1:T(2,128)(2,1)}), bf16[1,96,3,2,768]{4,3,2,0,1:T(2,128)(2,1)S(1)}, u32[]{:S(2)}, u32[]{:S(2)}) async-start(bf16[1,96,3,2,768]{4,3,2,0,1:T(2,128)(2,1)} %copy.152), calls=%async_computation.1 | async-start | bytes 1769472 | tf_op jit(solution)/shard_map/all_to_all | solution.py:142
  122.9 2.3 maximum_multiply_fusion
  125.3 2.9 fusion.39
  128.2 1.8 copy.163
  130.0 1.9 reshape.695
  131.9 1.6 fusion.45
  133.5 1.8 copy.165
  135.3 6.8 %all-to-all-done.1 = bf16[1,96,3,2,768]{4,3,2,0,1:T(2,128)(2,1)S(1)} async-done(((bf16[1,96,3,2,768]{4,3,2,0,1:T(2,128)(2,1)}), bf16[1,96,3,2,768]{4,3,2,0,1:T(2,128)(2,1)S(1)}, u32[]{:S(2)}, u32[]{:S(2)}) %all-to-all-start.1) | async-done | bytes 884768 | tf_op jit(solution)/shard_map/all_to_all | solution.py:142
  142.1 6.9 %all-to-all-start.3 = ((bf16[1,96,3,2,768]{4,3,2,0,1:T(2,128)(2,1)}), bf16[1,96,3,2,768]{4,3,2,0,1:T(2,128)(2,1)}, u32[]{:S(2)}, u32[]{:S(2)}) async-start(bf16[1,96,3,2,768]{4,3,2,0,1:T(2,128)(2,1)} %copy.165), calls=%async_computation.3 | async-start | bytes 1769472 | tf_op jit(solution)/shard_map/all_to_all | solution.py:155
  149.1 260.8 %all-reduce.2.cloned.1.call-done = f32[297984]{0:T(1024)} async-done(((f32[297984]{0:T(1024)}), f32[297984]{0:T(1024)}) %all-reduce.2.cloned.1.call-update) | async-done | bytes 1191952 | tf_op jit(solution)/shard_map/psum | solution.py:161
  409.9 1.3 fusion.121
  416.1 1.4 fusion.37
  417.5 1.8 copy.166
  420.7 1.6 fusion.33
  (147 shorter events, 27.3 us)
Async XLA Ops:
  8.2 17.2 %copy-start = (bf16[1,3,180,768]{3,2,1,0:T(8,128)(2,1)S(1)}, bf16[1,3,180,768]{3,2,1,0:T(8,128)(2,1)}, u32[]{:S(2)}) copy-start(bf16[1,3,180,768]{3,2,1,0:T(8,128)(2,1)} %param.6) | copy-start | bytes 2488324
  11.8 36.7 %all-to-all-start.2 = ((bf16[1,3,96,2,768]{4,3,1,0,2:T(2,128)(2,1)}), bf16[1,3,96,2,768]{4,3,1,0,2:T(2,128)(2,1)S(1)}, u32[]{:S(2)}, u32[]{:S(2)}) async-start(bf16[1,3,96,2,768]{4,3,1,0,2:T(2,128)(2,1)} %copy.155), calls=%async_computation.2 | async-start | bytes 1769472 | tf_op jit(solution)/shard_map/all_to_all | solution.py:147
  26.1 1.7 copy-start.25
  26.7 1.1 copy-start.23
  28.9 26.7 %copy-start.28 = (f32[2,768]{1,0:T(2,128)S(1)}, f32[2,768]{1,0:T(2,128)}, u32[]{:S(2)}) copy-start(f32[2,768]{1,0:T(2,128)} %param.9) | copy-start | bytes 18436
  48.4 28.1 %all-to-all-start = ((bf16[32,1,3,3,2,768]{5,4,3,2,1,0:T(2,128)(2,1)}), bf16[32,1,3,3,2,768]{5,4,3,2,1,0:T(2,128)(2,1)S(1)}, u32[]{:S(2)}, u32[]{:S(2)}) async-start(bf16[32,1,3,3,2,768]{5,4,3,2,1,0:T(2,128)(2,1)} %copy.145), calls=%async_computation | async-start | bytes 1769472 | tf_op jit(solution)/shard_map/all_to_all | solution.py:133
  56.7 5.9 %copy-start.30 = (f32[3]{0:T(128)}, f32[3]{0:T(128)S(1)}, u32[]{:S(2)}) copy-start(f32[3]{0:T(128)S(1)} %compare_select_fusion) | copy-start | bytes 40
  57.1 5.4 %copy-start.9 = (bf16[96,1,96,2]{2,0,3,1:T(8,128)(2,1)}, bf16[96,1,96,2]{2,0,3,1:T(8,128)(2,1)S(1)}, u32[]{:S(2)}) copy-start(bf16[96,1,96,2]{2,0,3,1:T(8,128)(2,1)S(1)} %get-tuple-element.22) | copy-start | bytes 110596
  58.1 32.4 %copy-start.4 = (bf16[8,1,96,2,96]{2,4,1,3,0:T(8,128)(2,1)}, bf16[8,1,96,2,96]{2,4,1,3,0:T(8,128)(2,1)S(1)}, u32[]{:S(2)}) copy-start(bf16[8,1,96,2,96]{2,4,1,3,0:T(8,128)(2,1)S(1)} %get-tuple-element.19) | copy-start | bytes 884740
  66.3 15.6 %copy-start.22 = (f32[2,8,96]{2,0,1:T(2,128)S(1)}, f32[2,8,96]{2,0,1:T(2,128)}, u32[]{:S(2)}) copy-start(f32[2,8,96]{2,0,1:T(2,128)} %copy.148) | copy-start | bytes 18436
  88.9 9.1 %copy-start.1 = (f32[8,2,96,96,3,1]{2,3,5,4,1,0:T(8,128)}, f32[8,2,96,96,3,1]{2,3,5,4,1,0:T(8,128)S(1)}, u32[]{:S(2)}) copy-start(f32[8,2,96,96,3,1]{2,3,5,4,1,0:T(8,128)S(1)} %get-tuple-element.35) | copy-start | bytes 5308420
  89.7 1.0 copy-start.5
  90.7 7.2 %copy-start.8 = (bf16[96,3,2,8,96]{4,3,0,2,1:T(8,128)(2,1)S(1)}, bf16[96,3,2,8,96]{4,3,0,2,1:T(8,128)(2,1)}, u32[]{:S(2)}) copy-start(bf16[96,3,2,8,96]{4,3,0,2,1:T(8,128)(2,1)} %reshape.653) | copy-start | bytes 2654212
  99.9 2.2 copy-start.7
  108.7 2.1 copy-start.10
  108.7 2.1 copy-start.29
  108.7 2.1 copy-start.31
  111.3 9.2 %copy-start.6 = (f32[1,8,96,96]{3,2,1,0:T(8,128)S(1)}, f32[1,8,96,96]{3,2,1,0:T(8,128)}, u32[]{:S(2)}) copy-start(f32[1,8,96,96]{3,2,1,0:T(8,128)} %fusion.84) | copy-start | bytes 884740
  113.8 9.1 %copy-start.3 = (f32[147456]{0:T(1024)S(1)}, f32[147456]{0:T(1024)}, u32[]{:S(2)}) copy-start(f32[147456]{0:T(1024)} %reshape.666) | copy-start | bytes 1769476
  113.8 28.3 %all-to-all-start.1 = ((bf16[1,96,3,2,768]{4,3,2,0,1:T(2,128)(2,1)}), bf16[1,96,3,2,768]{4,3,2,0,1:T(2,128)(2,1)S(1)}, u32[]{:S(2)}, u32[]{:S(2)}) async-start(bf16[1,96,3,2,768]{4,3,2,0,1:T(2,128)(2,1)} %copy.152), calls=%async_computation.1 | async-start | bytes 1769472 | tf_op jit(solution)/shard_map/all_to_all | solution.py:142
  120.5 289.4 %all-reduce.2.cloned.1.call-start = ((), (), s32[]{:S(2)}) async-start(), calls=%async_computation.4 | async-start | bytes 2383872 | tf_op jit(solution)/shard_map/psum | solution.py:161
  121.6 3.7 copy-start.12
  122.9 2.4 copy-start.13
  128.2 3.7 copy-start.11
  142.1 275.3 %all-to-all-start.3 = ((bf16[1,96,3,2,768]{4,3,2,0,1:T(2,128)(2,1)}), bf16[1,96,3,2,768]{4,3,2,0,1:T(2,128)(2,1)}, u32[]{:S(2)}, u32[]{:S(2)}) async-start(bf16[1,96,3,2,768]{4,3,2,0,1:T(2,128)(2,1)} %copy.165), calls=%async_computation.3 | async-start | bytes 1769472 | tf_op jit(solution)/shard_map/all_to_all | solution.py:155
  411.2 4.8 %copy-start.15 = (bf16[180,96,1]{1,0,2:T(8,128)(2,1)S(1)}, bf16[180,96,1]{1,0,2:T(8,128)(2,1)}, u32[]{:S(2)}) copy-start(bf16[180,96,1]{1,0,2:T(8,128)(2,1)} %copy-done.14) | copy-start | bytes 103684
  411.2 4.8 %copy-start.17 = (bf16[180,96,1]{1,0,2:T(8,128)(2,1)S(1)}, bf16[180,96,1]{1,0,2:T(8,128)(2,1)}, u32[]{:S(2)}) copy-start(bf16[180,96,1]{1,0,2:T(8,128)(2,1)} %copy-done.16) | copy-start | bytes 103684
  411.2 4.8 %copy-start.24 = (f32[3,180]{1,0:T(4,128)S(1)}, f32[3,180]{1,0:T(4,128)}, u32[]{:S(2)}) copy-start(f32[3,180]{1,0:T(4,128)} %copy-done.23) | copy-start | bytes 6484
  416.0 3.2 copy-start.2
  416.1 3.2 copy-start.19
  416.1 3.2 copy-start.21
  416.1 3.2 copy-start.27
  (5 other events, 3.3 us)
Sparse Core Ops, SparseCore 0:
  126.4 283.4 all-reduce.1
